TPU v7x, 32 devices: a whole 2x2x4 slice. The times are simulated.
32 devices in a mesh: mem: 4 (over y, core), sub: 8 (over z, x).
Axes of the slice: x: 2, y: 2, z: 4, core: 2. Of those that a mesh axis runs over, the one named last changes fastest.
Arguments:
- prior_sample_array: float32 [80, 8, 24, 512], P('mem', 'sub'), may hold values from -6 to 6
- courant_x: float32 [8, 512], P('sub'), may hold values from -0.3 to 0.3
- courant_y: float32 [8, 512], P('sub'), may hold values from -0.3 to 0.3
- diffusion: float32 [8, 512], P('sub'), may hold values from 0.02 to 0.09
- obs_cell: int32 [4, 128], replicated, may hold values from 0 to 4095
- obs_value: float32 [4, 128], replicated, may hold values from -6 to 6
- obs_error: float32 [4, 128], replicated, may hold values from 0.2 to 1
- obs_weight: float32 [4, 128, 24], replicated, may hold values from -1.25 to 1.25
- taper_radius: float32 [4, 128], replicated, may hold values from 64 to 256
Outputs:
- analysis: float32 [80, 8, 24, 512], P(None, 'sub', None, 'mem')
All inputs are finite; a program needn't handle non-finite values.
Results may differ from a plain program's by a relative error of at most 0.0003.
Values sent between devices are 32-bit elements; how exact they have to be, the bound alone decides.
No kernel may reach another device: no remote copies, remote signals or barrier semaphores. Data moves between devices by JAX's collectives and lax.ppermute only.
A program may use at most 64 MiB of HBM per device.

v0:
```python
import jax
import jax.numpy as jnp
from jax import lax
from jax.sharding import PartitionSpec as P

highest = lax.Precision.HIGHEST


def padded_2(shard, sides, width):
    for axis, dim in sides:
        size, length = (lax.axis_size(axis), shard.shape[dim])
        up = [(i, (i + 1) % size) for i in range(size - 1)]
        down = [(j, i) for i, j in up]
        last = lax.slice_in_dim(shard, length - width, length, axis=dim)
        first = lax.slice_in_dim(shard, 0, width, axis=dim)
        before = lax.ppermute(last, axis, up)
        after = lax.ppermute(first, axis, down)
        shard = jnp.concatenate([before, shard, after], axis=dim)
    return shard


def gaspari(delta_row, delta_col, cutoff_radius, width):
    cyclic_shifted = (delta_col + width // 2) % width - width // 2
    row_dist = delta_row.astype(jnp.float32)
    col_dist = cyclic_shifted.astype(jnp.float32)
    ratio = jnp.sqrt(row_dist * row_dist + col_dist * col_dist) / cutoff_radius
    inner = (((-0.25 * ratio + 0.5) * ratio + 0.625) * ratio - 5.0 / 3.0) * ratio * ratio + 1.0
    bounded = jnp.maximum(ratio, 1.0)
    outer = (
        ((((ratio / 12.0 - 0.5) * ratio + 0.625) * ratio + 5.0 / 3.0) * ratio - 5.0) * ratio
        + 4.0
        - 2.0 / (3.0 * bounded)
    )
    return jnp.where(ratio <= 1.0, inner, jnp.where(ratio < 2.0, outer, 0.0))


def carried_quantity(
    center,
    west_cells,
    east_cells,
    north_cells,
    southern_neighbours,
    flow_x,
    meridional_velocity,
    mixing,
):
    result = (
        center
        - jnp.maximum(flow_x, 0.0) * (center - west_cells)
        - jnp.minimum(flow_x, 0.0) * (east_cells - center)
    )
    result = (
        result
        - jnp.maximum(meridional_velocity, 0.0) * (center - southern_neighbours)
        - jnp.minimum(meridional_velocity, 0.0) * (north_cells - center)
    )
    return result + mixing * (
        east_cells + west_cells + north_cells + southern_neighbours - 4.0 * center
    )


def obs_factors(obs_prior, obs_value, obs_error):
    members = obs_prior.shape[1]
    average = jnp.mean(obs_prior, axis=1)
    anomaly = obs_prior - average[:, None]
    covariance = jnp.dot(anomaly, anomaly.T, precision=highest) / (members - 1) + jnp.diag(
        obs_error
    )
    factor = jnp.linalg.cholesky(covariance)
    innovation = (obs_value - average)[:, None]
    midpoint_values = lax.linalg.triangular_solve(factor, innovation, left_side=True, lower=True)
    solved = lax.linalg.triangular_solve(
        factor, midpoint_values, left_side=True, lower=True, transpose_a=True
    )
    shifted = factor + jnp.diag(jnp.sqrt(obs_error))
    reduced = lax.linalg.triangular_solve(shifted, anomaly, left_side=True, lower=True)
    squared = lax.linalg.triangular_solve(
        factor, reduced, left_side=True, lower=True, transpose_a=True
    )
    return (anomaly, solved - squared)


def local_prior(existing_grid_values, obs_rows, obs_cols, weights, row_start, col_start):
    rows_dev = existing_grid_values.shape[1]
    cols_dev = existing_grid_values.shape[3]
    local_rows = obs_rows - row_start
    local_cols = obs_cols - col_start
    owned = (
        (local_rows >= 0) & (local_rows < rows_dev) & (local_cols >= 0) & (local_cols < cols_dev)
    )
    picked = existing_grid_values[
        :, jnp.clip(local_rows, 0, rows_dev - 1), :, jnp.clip(local_cols, 0, cols_dev - 1)
    ]
    values = jnp.einsum("kmc,kc->km", picked, weights, precision=highest)
    return jnp.where(owned[:, None], values, 0.0)


def apply_update(existing_grid_values, obs_anomaly, coeffs, taper_cells, members):
    average = jnp.mean(existing_grid_values, axis=0)
    anomaly = existing_grid_values - average[None]
    cross_cov = jnp.einsum("mrcx,km->rcxk", anomaly, obs_anomaly, precision=highest) / (members - 1)
    gain = cross_cov * taper_cells[:, None, :, :]
    return existing_grid_values + jnp.einsum("rcxk,km->mrcx", gain, coeffs, precision=highest)


def shards(
    prior_sample_array,
    courant_x,
    courant_y,
    diffusion,
    obs_cell,
    obs_value,
    obs_error,
    obs_weight,
    taper_radius,
):
    width = courant_x.shape[1]
    rows_dev = prior_sample_array.shape[1]
    cols_dev = width // lax.axis_size("mem")
    members = prior_sample_array.shape[0] * lax.axis_size("mem")
    col_start = lax.axis_index("mem") * cols_dev
    row_start = lax.axis_index("sub") * rows_dev
    padded = padded_2(prior_sample_array, (("sub", 1),), 1)
    propagated_grids = carried_quantity(
        prior_sample_array,
        jnp.roll(prior_sample_array, 1, axis=3),
        jnp.roll(prior_sample_array, -1, axis=3),
        padded[:, 2:],
        padded[:, :-2],
        courant_x[:, None, :],
        courant_y[:, None, :],
        diffusion[:, None, :],
    )
    existing_grid_values = lax.all_to_all(
        propagated_grids, "mem", split_axis=3, concat_axis=0, tiled=True
    )
    row_ids = row_start + jnp.arange(rows_dev, dtype=jnp.int32)
    col_ids = col_start + jnp.arange(cols_dev, dtype=jnp.int32)
    obs_rows = obs_cell // width
    obs_cols = obs_cell % width
    batches = obs_cell.shape[0]

    def taper_cells(batch_index):
        return gaspari(
            row_ids[:, None, None] - obs_rows[batch_index][None, None, :],
            col_ids[None, :, None] - obs_cols[batch_index][None, None, :],
            taper_radius[batch_index][None, None, :],
            width,
        )

    for batch_index in range(batches):
        obs_prior = lax.psum(
            local_prior(
                existing_grid_values,
                obs_rows[batch_index],
                obs_cols[batch_index],
                obs_weight[batch_index],
                row_start,
                col_start,
            ),
            ("mem", "sub"),
        )
        obs_anomaly, coeffs = obs_factors(obs_prior, obs_value[batch_index], obs_error[batch_index])
        existing_grid_values = apply_update(
            existing_grid_values, obs_anomaly, coeffs, taper_cells(batch_index), members
        )
    return existing_grid_values


def solution(mesh):
    return jax.shard_map(
        shards,
        mesh=mesh,
        in_specs=(
            P("mem", "sub", None, None),
            P("sub", None),
            P("sub", None),
            P("sub", None),
            P(),
            P(),
            P(),
            P(),
            P(),
        ),
        out_specs=P(None, "sub", None, "mem"),
        check_vma=False,
    )
```

profile of v0, /device:TPU:0, one launch (start us, length us, event | category | flops | bytes accessed | tf_op | source)
XLA Modules:
  0.0 428.5 jit_solution(3687478982285887635)
XLA Ops:
  0.0 5.9 %collective-permute-start = (f32[20,1,24,512]{3,2,1,0:T(8,128)}, f32[20,1,24,512]{3,2,1,0:T(8,128)}, u32[]{:S(2)}, u32[]{:S(2)}) collective-permute-start(f32[20,1,24,512]{3,2,1,0:T(8,128)} %param.18), channel_id=1, source_target_pairs={{0,1},{1,2},{2,3},{3,4},{4,5},{5,6},{6,7},{8,9},{9,10},{10,11},{11... | collective-permute-start | bytes 2949128 | tf_op jit(solution)/shard_map/ppermute | solution.py:16
  5.9 1.3 collective-permute-start.1
  7.2 1.4 slice_bitcast_fusion.5
  8.6 1.4 fusion.183
  10.1 0.7 broadcast_maximum_fusion
  10.8 0.7 broadcast_maximum_fusion.1
  11.4 0.7 add_select_fusion.5
  12.2 0.8 slice_bitcast_fusion
  12.9 1.2 fusion.184
  14.5 32.9 %collective-permute-done = f32[20,1,24,512]{3,2,1,0:T(8,128)} collective-permute-done((f32[20,1,24,512]{3,2,1,0:T(8,128)}, f32[20,1,24,512]{3,2,1,0:T(8,128)}, u32[]{:S(2)}, u32[]{:S(2)}) %collective-permute-start) | collective-permute-done | bytes 983072 | tf_op jit(solution)/shard_map/ppermute | solution.py:16
  47.4 0.9 copy-done.10
  48.3 2.4 multiply_add_fusion
  50.7 4.3 copy.87
  54.9 6.5 %reshape.1524 = f32[4,1,61440]{2,1,0:T(1,128)} reshape(f32[512,1,20,24]{3,2,1,0:T(8,128)} %bitcast.330) | data formatting | bytes 1966080
  61.5 4.1 all-to-all-start
  65.6 0.7 copy.126
  66.3 0.7 copy.127
  67.2 0.6 fusion.152
  68.4 10.9 %all-to-all-done = f32[4,1,61440]{2,1,0:T(1,128)S(1)} async-done(((f32[4,1,61440]{2,1,0:T(1,128)}), f32[4,1,61440]{2,1,0:T(1,128)S(1)}, u32[]{:S(2)}, u32[]{:S(2)}) %all-to-all-start) | async-done | bytes 983072 | tf_op jit(solution)/shard_map/all_to_all | solution.py:134
  79.8 3.5 reduce.20
  83.3 6.0 %reshape.1525 = f32[512,1,20,24]{3,2,1,0:T(8,128)} reshape(f32[4,61440]{1,0:T(4,128)S(1)} %reduce.20) | data formatting | bytes 1966080
  89.4 5.6 %copy.88 = f32[20,1,24,512]{3,1,2,0:T(1,128)S(1)} copy(f32[20,1,24,512]{2,0,1,3:T(8,128)} %bitcast.331) | data formatting | bytes 1966080 | tf_op jit(solution)/shard_map/all_to_all | solution.py:134
  95.0 0.9 copy-done.9
  95.9 0.6 copy.91
  96.8 0.8 gather_fusion
  97.7 1.4 multiply_reduce_fusion.3
  99.2 41.8 %psum.28 = f32[128,80]{0,1:T(8,128)S(1)} all-reduce(f32[128,80]{0,1:T(8,128)S(1)} %broadcast_select_fusion.3), channel_id=1, replica_groups=mesh['mem'=4,'sub'=8] {'mem','sub'}, use_global_device_ids=true, to_apply=%region_0.1 | all-reduce | flops 10240 | bytes 81920 | tf_op jit(solution)/shard_map/psum | solution.py:152
  141.0 1.4 reduce_sum.73
  143.0 11.7 %cholesky.74 = f32[128,128]{1,0:T(8,128)S(1)} custom-call(f32[128,128]{1,0:T(8,128)S(1)} %copy.93), custom_call_target="Cholesky" | custom-call | tf_op jit(solution)/shard_map/jit(cholesky)/cholesky | solution.py:69
  154.7 0.6 compare_reduce_fusion.3
  155.4 0.7 select_bitcast_fusion.7
  156.1 9.8 %custom-call.36 = f32[1,128,128]{1,2,0:T(8,128)S(1)} custom-call(f32[1,128,128]{2,1,0:T(8,128)S(1)} %get-tuple-element.21), custom_call_target="InvertDiagBlocksLowerTriangular" | custom-call | tf_op jit(solution)/shard_map/triangular_solve/custom-call.3 | solution.py:76
  166.1 9.8 %custom-call.35 = f32[1,128,128]{1,2,0:T(8,128)S(1)} custom-call(f32[1,128,128]{2,1,0:T(8,128)S(1)} %get-tuple-element.20), custom_call_target="InvertDiagBlocksLowerTriangular" | custom-call | tf_op jit(solution)/shard_map/triangular_solve/custom-call.2 | solution.py:72
  176.4 2.6 fusion.31
  179.3 2.8 fusion.186
  183.0 0.8 gather_fusion.1
  184.5 40.4 %psum.29 = f32[128,80]{0,1:T(8,128)S(1)} all-reduce(f32[128,80]{0,1:T(8,128)S(1)} %broadcast_select_fusion.2), channel_id=1, replica_groups=mesh['mem'=4,'sub'=8] {'mem','sub'}, use_global_device_ids=true, to_apply=%region_5.11 | all-reduce | flops 10240 | bytes 81920 | tf_op jit(solution)/shard_map/psum | solution.py:152
  225.5 11.7 %cholesky.85 = f32[128,128]{1,0:T(8,128)S(1)} custom-call(f32[128,128]{1,0:T(8,128)S(1)} %copy.98), custom_call_target="Cholesky" | custom-call | tf_op jit(solution)/shard_map/jit(cholesky)/cholesky | solution.py:69
  237.3 0.7 compare_reduce_fusion.2
  238.0 0.7 select_bitcast_fusion.5
  238.7 9.8 %custom-call.40 = f32[1,128,128]{1,2,0:T(8,128)S(1)} custom-call(f32[1,128,128]{2,1,0:T(8,128)S(1)} %get-tuple-element.19), custom_call_target="InvertDiagBlocksLowerTriangular" | custom-call | tf_op jit(solution)/shard_map/triangular_solve/custom-call.3 | solution.py:76
  248.7 9.8 %custom-call.39 = f32[1,128,128]{1,2,0:T(8,128)S(1)} custom-call(f32[1,128,128]{2,1,0:T(8,128)S(1)} %get-tuple-element.18), custom_call_target="InvertDiagBlocksLowerTriangular" | custom-call | tf_op jit(solution)/shard_map/triangular_solve/custom-call.2 | solution.py:72
  258.9 2.6 fusion.37
  261.8 1.9 fusion.187
  263.7 0.5 copy.99
  264.7 0.8 gather_fusion.2
  266.2 40.3 %psum.30 = f32[128,80]{0,1:T(8,128)S(1)} all-reduce(f32[128,80]{0,1:T(8,128)S(1)} %broadcast_select_fusion.1), channel_id=1, replica_groups=mesh['mem'=4,'sub'=8] {'mem','sub'}, use_global_device_ids=true, to_apply=%region_8.14 | all-reduce | flops 10240 | bytes 81920 | tf_op jit(solution)/shard_map/psum | solution.py:152
  307.1 11.7 %cholesky.96 = f32[128,128]{1,0:T(8,128)S(1)} custom-call(f32[128,128]{1,0:T(8,128)S(1)} %copy.101), custom_call_target="Cholesky" | custom-call | tf_op jit(solution)/shard_map/jit(cholesky)/cholesky | solution.py:69
  318.8 0.7 compare_reduce_fusion.1
  319.5 0.7 select_bitcast_fusion.3
  320.2 9.8 %custom-call.44 = f32[1,128,128]{1,2,0:T(8,128)S(1)} custom-call(f32[1,128,128]{2,1,0:T(8,128)S(1)} %get-tuple-element.17), custom_call_target="InvertDiagBlocksLowerTriangular" | custom-call | tf_op jit(solution)/shard_map/triangular_solve/custom-call.3 | solution.py:76
  330.2 9.8 %custom-call.43 = f32[1,128,128]{1,2,0:T(8,128)S(1)} custom-call(f32[1,128,128]{2,1,0:T(8,128)S(1)} %get-tuple-element.16), custom_call_target="InvertDiagBlocksLowerTriangular" | custom-call | tf_op jit(solution)/shard_map/triangular_solve/custom-call.2 | solution.py:72
  340.4 2.6 fusion.35
  343.3 1.9 fusion.188
  346.2 0.8 gather_fusion.3
  347.7 40.6 %psum.31 = f32[128,80]{0,1:T(8,128)S(1)} all-reduce(f32[128,80]{0,1:T(8,128)S(1)} %broadcast_select_fusion), channel_id=1, replica_groups=mesh['mem'=4,'sub'=8] {'mem','sub'}, use_global_device_ids=true, to_apply=%region_11.17 | all-reduce | flops 10240 | bytes 81920 | tf_op jit(solution)/shard_map/psum | solution.py:152
  388.9 11.7 %cholesky.107 = f32[128,128]{1,0:T(8,128)S(1)} custom-call(f32[128,128]{1,0:T(8,128)S(1)} %copy.104), custom_call_target="Cholesky" | custom-call | tf_op jit(solution)/shard_map/jit(cholesky)/cholesky | solution.py:69
  400.7 0.7 compare_reduce_fusion
  401.4 0.8 select_bitcast_fusion.1
  402.2 9.8 %custom-call.48 = f32[1,128,128]{1,2,0:T(8,128)S(1)} custom-call(f32[1,128,128]{2,1,0:T(8,128)S(1)} %get-tuple-element.15), custom_call_target="InvertDiagBlocksLowerTriangular" | custom-call | tf_op jit(solution)/shard_map/triangular_solve/custom-call.3 | solution.py:76
  412.2 9.8 %custom-call.47 = f32[1,128,128]{1,2,0:T(8,128)S(1)} custom-call(f32[1,128,128]{2,1,0:T(8,128)S(1)} %get-tuple-element.14), custom_call_target="InvertDiagBlocksLowerTriangular" | custom-call | tf_op jit(solution)/shard_map/triangular_solve/custom-call.2 | solution.py:72
  422.4 2.6 fusion.33
  425.3 1.7 fusion.20
  427.0 1.2 copy.105
  (129 shorter events, 11.8 us)
Async XLA Ops:
  0.0 14.1 %copy-start.8 = (f32[20,1,24,512]{3,2,1,0:T(8,128)S(1)}, f32[20,1,24,512]{3,2,1,0:T(8,128)}, u32[]{:S(2)}) copy-start(f32[20,1,24,512]{3,2,1,0:T(8,128)} %param.18) | copy-start | bytes 2949124
  0.0 47.4 %collective-permute-start = (f32[20,1,24,512]{3,2,1,0:T(8,128)}, f32[20,1,24,512]{3,2,1,0:T(8,128)}, u32[]{:S(2)}, u32[]{:S(2)}) collective-permute-start(f32[20,1,24,512]{3,2,1,0:T(8,128)} %param.18), channel_id=1, source_target_pairs={{0,1},{1,2},{2,3},{3,4},{4,5},{5,6},{6,7},{8,9},{9,10},{10,11},{11... | collective-permute-start | bytes 2949128 | tf_op jit(solution)/shard_map/ppermute | solution.py:16
  5.9 41.4 %collective-permute-start.1 = (f32[20,1,24,512]{3,2,1,0:T(8,128)}, f32[20,1,24,512]{3,2,1,0:T(8,128)S(1)}, u32[]{:S(2)}, u32[]{:S(2)}) collective-permute-start(f32[20,1,24,512]{3,2,1,0:T(8,128)} %param.18), channel_id=1, source_target_pairs={{1,0},{2,1},{3,2},{4,3},{5,4},{6,5},{7,6},{9,8},{10,9},{11,10},{12... | collective-permute-start | bytes 2949128 | tf_op jit(solution)/shard_map/ppermute | solution.py:17
  14.1 34.2 %copy-start.15 = (f32[1,512]{1,0:T(1,128)S(1)}, f32[1,512]{1,0:T(1,128)}, u32[]{:S(2)}) copy-start(f32[1,512]{1,0:T(1,128)} %param.21) | copy-start | bytes 6148
  47.4 0.9 copy-start.10
  61.5 6.4 %copy-start.28 = (f32[4,128]{1,0:T(4,128)S(1)}, f32[4,128]{1,0:T(4,128)}, u32[]{:S(2)}) copy-start(f32[4,128]{1,0:T(4,128)} %param.26) | copy-start | bytes 6148
  61.5 17.8 %all-to-all-start = ((f32[4,1,61440]{2,1,0:T(1,128)}), f32[4,1,61440]{2,1,0:T(1,128)S(1)}, u32[]{:S(2)}, u32[]{:S(2)}) async-start(f32[4,1,61440]{2,1,0:T(1,128)} %reshape.1524), calls=%async_computation | async-start | bytes 1966080 | tf_op jit(solution)/shard_map/all_to_all | solution.py:134
  94.9 0.9 copy-start.9
  95.9 1.0 copy-start.6
  97.7 1.5 copy-start.19
  97.7 44.8 %copy-start.27 = (f32[128]{0:T(128)S(1)}, f32[128]{0:T(128)}, u32[]{:S(2)}) copy-start(f32[128]{0:T(128)} %get-tuple-element.52) | copy-start | bytes 1540
  97.7 57.7 %copy-start.26 = (f32[128]{0:T(128)S(1)}, f32[128]{0:T(128)}, u32[]{:S(2)}) copy-start(f32[128]{0:T(128)} %get-tuple-element.49) | copy-start | bytes 1540
  99.1 76.8 %copy-start.13 = (f32[4,128]{1,0:T(4,128)S(1)}, f32[4,128]{1,0:T(4,128)}, u32[]{:S(2)}) copy-start(f32[4,128]{1,0:T(4,128)} %param.23) | copy-start | bytes 6148
  99.1 77.2 %copy-start.7 = (f32[4,20,1,24,128]{4,3,1,0,2:T(8,128)S(1)}, f32[4,20,1,24,128]{4,3,1,0,2:T(8,128)}, u32[]{:S(2)}) copy-start(f32[4,20,1,24,128]{4,3,1,0,2:T(8,128)} %copy-done.6) | copy-start | bytes 2949124
  182.1 0.9 copy-start.2
  183.0 0.8 copy-start.11
  183.9 0.7 copy-start.18
  183.9 41.1 %copy-start.25 = (f32[128]{0:T(128)S(1)}, f32[128]{0:T(128)}, u32[]{:S(2)}) copy-start(f32[128]{0:T(128)} %get-tuple-element.51) | copy-start | bytes 1540
  183.9 54.1 %copy-start.24 = (f32[128]{0:T(128)S(1)}, f32[128]{0:T(128)}, u32[]{:S(2)}) copy-start(f32[128]{0:T(128)} %get-tuple-element.48) | copy-start | bytes 1540
  183.9 75.0 %copy-start.12 = (f32[24,128]{1,0:T(8,128)S(1)}, f32[24,128]{1,0:T(8,128)}, u32[]{:S(2)}) copy-start(f32[24,128]{1,0:T(8,128)} %get-tuple-element.64) | copy-start | bytes 36868
  183.9 75.0 %copy-start.3 = (f32[80,24,128]{2,0,1:T(8,128)S(1)}, f32[80,24,128]{2,0,1:T(8,128)}, u32[]{:S(2)}) copy-start(f32[80,24,128]{2,0,1:T(8,128)} %copy-done.2) | copy-start | bytes 2949124
  263.7 0.9 copy-start.4
  265.5 0.7 copy-start.17
  265.5 41.0 %copy-start.23 = (f32[128]{0:T(128)S(1)}, f32[128]{0:T(128)}, u32[]{:S(2)}) copy-start(f32[128]{0:T(128)} %get-tuple-element.53) | copy-start | bytes 1540
  265.5 54.0 %copy-start.22 = (f32[128]{0:T(128)S(1)}, f32[128]{0:T(128)}, u32[]{:S(2)}) copy-start(f32[128]{0:T(128)} %get-tuple-element.47) | copy-start | bytes 1540
  265.5 74.9 %copy-start.5 = (f32[80,24,128]{2,0,1:T(8,128)S(1)}, f32[80,24,128]{2,0,1:T(8,128)}, u32[]{:S(2)}) copy-start(f32[80,24,128]{2,0,1:T(8,128)} %copy-done.4) | copy-start | bytes 2949124
  345.3 0.9 copy-start
  347.1 0.7 copy-start.16
  347.1 41.3 %copy-start.21 = (f32[128]{0:T(128)S(1)}, f32[128]{0:T(128)}, u32[]{:S(2)}) copy-start(f32[128]{0:T(128)} %get-tuple-element.50) | copy-start | bytes 1540
  347.1 54.3 %copy-start.20 = (f32[128]{0:T(128)S(1)}, f32[128]{0:T(128)}, u32[]{:S(2)}) copy-start(f32[128]{0:T(128)} %get-tuple-element.46) | copy-start | bytes 1540
  347.1 74.9 %copy-start.14 = (f32[4,128]{1,0:T(4,128)S(1)}, f32[4,128]{1,0:T(4,128)}, u32[]{:S(2)}) copy-start(f32[4,128]{1,0:T(4,128)} %param.23) | copy-start | bytes 6148
  347.1 75.3 %copy-start.1 = (f32[80,24,128]{2,0,1:T(8,128)S(1)}, f32[80,24,128]{2,0,1:T(8,128)}, u32[]{:S(2)}) copy-start(f32[80,24,128]{2,0,1:T(8,128)} %copy-done) | copy-start | bytes 2949124
where the time goes:
time: 432 us; the launch traced here: 428 us
  blocking collectives  163 us (38%)
  other arithmetic  145 us (34%)
  waiting for transfers between devices  43.8 us (10%)
  local copies, waits for them, and re-layouts  41.1 us (10%)
  matrix products  23.1 us (5%)
  starting transfers between devices  11.3 us (3%)
    psum x4, blocking collectives, shards(): lax.psum(local_prior(existing_grid_values, obs_rows[batch_index], obs_col...  163 us
    another operation x12, other arithmetic, obs_factors(): factor = jnp.linalg.cholesky(covariance)  49.7 us
    another operation x8, other arithmetic, obs_factors(): lax.linalg.triangular_solve(factor, midpoint_values, left_side=True, lowe...  42.2 us
    another operation x4, other arithmetic, obs_factors(): lax.linalg.triangular_solve(shifted, anomaly, left_side=True, lower=True)  39.2 us
    ppermute x1, waiting for transfers between devices, padded_2(): before = lax.ppermute(last, axis, up)  32.9 us
    unnamed x64, local copies, waits for them, and re-layouts  17.7 us
    all_to_all x1, waiting for transfers between devices, shards(): lax.all_to_all(propagated_grids, 'mem', split_axis=3, concat_axis=0, tile...  10.9 us
    dot_general x4, matrix products, apply_update(): jnp.einsum('mrcx,km->rcxk', anomaly, obs_anomaly, precision=highest)  10.5 us
  transfers between devices with their start and end apart: 3, of which 2 were waited for; matrix products, arithmetic and copies ran while one was open for 2% of the time, Pallas kernels for 0%

commit v1 on v0

--- a/solution.py
+++ b/solution.py
@@ -149,17 +149,16 @@
         )
 
     for batch_index in range(batches):
-        obs_prior = lax.psum(
-            local_prior(
-                existing_grid_values,
-                obs_rows[batch_index],
-                obs_cols[batch_index],
-                obs_weight[batch_index],
-                row_start,
-                col_start,
-            ),
-            ("mem", "sub"),
+        obs_prior = local_prior(
+            existing_grid_values,
+            obs_rows[batch_index],
+            obs_cols[batch_index],
+            obs_weight[batch_index],
+            row_start,
+            col_start,
         )
+        for mesh_axis in ("sub", "mem"):
+            obs_prior = lax.psum(obs_prior, mesh_axis)
         obs_anomaly, coeffs = obs_factors(obs_prior, obs_value[batch_index], obs_error[batch_index])
         existing_grid_values = apply_update(
             existing_grid_values, obs_anomaly, coeffs, taper_cells(batch_index), members

time: 432 us -> 451 us (1.044)
  blocking collectives: 163 us -> 182 us
    psum x4 -> x8, blocking collectives: 163 us -> 182 us  [shards(): obs_prior = lax.psum(obs_prior, mesh_axis)]
where the time goes in v1:
time: 451 us; the launch traced here: 447 us
  blocking collectives  182 us (40%)
  other arithmetic  145 us (32%)
  waiting for transfers between devices  43.8 us (10%)
  local copies, waits for them, and re-layouts  41.1 us (9%)
  matrix products  23.1 us (5%)
  starting transfers between devices  11.3 us (3%)
    psum x8, blocking collectives, shards(): obs_prior = lax.psum(obs_prior, mesh_axis)  182 us
    another operation x12, other arithmetic, obs_factors(): factor = jnp.linalg.cholesky(covariance)  49.7 us
    another operation x8, other arithmetic, obs_factors(): lax.linalg.triangular_solve(factor, midpoint_values, left_side=True, lowe...  42.2 us
    another operation x4, other arithmetic, obs_factors(): lax.linalg.triangular_solve(shifted, anomaly, left_side=True, lower=True)  39.2 us
    ppermute x1, waiting for transfers between devices, padded_2(): before = lax.ppermute(last, axis, up)  32.9 us
    unnamed x64, local copies, waits for them, and re-layouts  17.7 us
    all_to_all x1, waiting for transfers between devices, shards(): lax.all_to_all(propagated_grids, 'mem', split_axis=3, concat_axis=0, tile...  10.9 us
    dot_general x4, matrix products, apply_update(): jnp.einsum('mrcx,km->rcxk', anomaly, obs_anomaly, precision=highest)  10.5 us
  transfers between devices with their start and end apart: 3, of which 2 were waited for; matrix products, arithmetic and copies ran while one was open for 2% of the time, Pallas kernels for 0%

profile of v1, /device:TPU:0, one launch (start us, length us, event | category | flops | bytes accessed | tf_op | source)
XLA Modules:
  0.0 447.5 jit_solution(12589792750603687523)
XLA Ops:
  0.0 5.9 %collective-permute-start = (f32[20,1,24,512]{3,2,1,0:T(8,128)}, f32[20,1,24,512]{3,2,1,0:T(8,128)}, u32[]{:S(2)}, u32[]{:S(2)}) collective-permute-start(f32[20,1,24,512]{3,2,1,0:T(8,128)} %param.18), channel_id=1, source_target_pairs={{0,1},{1,2},{2,3},{3,4},{4,5},{5,6},{6,7},{8,9},{9,10},{10,11},{11... | collective-permute-start | bytes 2949128 | tf_op jit(solution)/shard_map/ppermute | solution.py:16
  5.9 1.3 collective-permute-start.1
  7.2 1.4 slice_bitcast_fusion.5
  8.6 1.4 fusion.183
  10.1 0.7 broadcast_maximum_fusion
  10.8 0.7 broadcast_maximum_fusion.1
  11.4 0.7 add_select_fusion.5
  12.2 0.8 slice_bitcast_fusion
  12.9 1.2 fusion.184
  14.5 32.9 %collective-permute-done = f32[20,1,24,512]{3,2,1,0:T(8,128)} collective-permute-done((f32[20,1,24,512]{3,2,1,0:T(8,128)}, f32[20,1,24,512]{3,2,1,0:T(8,128)}, u32[]{:S(2)}, u32[]{:S(2)}) %collective-permute-start) | collective-permute-done | bytes 983072 | tf_op jit(solution)/shard_map/ppermute | solution.py:16
  47.4 0.9 copy-done.10
  48.3 2.4 multiply_add_fusion
  50.7 4.3 copy.87
  54.9 6.5 %reshape.1524 = f32[4,1,61440]{2,1,0:T(1,128)} reshape(f32[512,1,20,24]{3,2,1,0:T(8,128)} %bitcast.330) | data formatting | bytes 1966080
  61.5 4.1 all-to-all-start
  65.6 0.7 copy.126
  66.3 0.7 copy.127
  68.4 10.9 %all-to-all-done = f32[4,1,61440]{2,1,0:T(1,128)S(1)} async-done(((f32[4,1,61440]{2,1,0:T(1,128)}), f32[4,1,61440]{2,1,0:T(1,128)S(1)}, u32[]{:S(2)}, u32[]{:S(2)}) %all-to-all-start) | async-done | bytes 983072 | tf_op jit(solution)/shard_map/all_to_all | solution.py:134
  79.8 3.5 reduce.20
  83.3 6.0 %reshape.1525 = f32[512,1,20,24]{3,2,1,0:T(8,128)} reshape(f32[4,61440]{1,0:T(4,128)S(1)} %reduce.20) | data formatting | bytes 1966080
  89.4 5.6 %copy.88 = f32[20,1,24,512]{3,1,2,0:T(1,128)S(1)} copy(f32[20,1,24,512]{2,0,1,3:T(8,128)} %bitcast.331) | data formatting | bytes 1966080 | tf_op jit(solution)/shard_map/all_to_all | solution.py:134
  95.0 0.9 copy-done.9
  96.8 0.8 gather_fusion
  97.7 1.4 multiply_reduce_fusion.3
  99.2 37.9 %psum.56 = f32[128,80]{0,1:T(8,128)S(1)} all-reduce(f32[128,80]{0,1:T(8,128)S(1)} %broadcast_select_fusion.3), channel_id=1, replica_groups=mesh['mem'=4,'sub'=8] {'sub'}, use_global_device_ids=true, to_apply=%region_0.1 | all-reduce | flops 10240 | bytes 81920 | tf_op jit(solution)/shard_map/psum | solution.py:161
  137.1 10.7 %psum.57 = f32[128,80]{0,1:T(8,128)S(1)} all-reduce(f32[128,80]{0,1:T(8,128)S(1)} %psum.56), channel_id=1, replica_groups=mesh['mem'=4,'sub'=8] {'mem'}, use_global_device_ids=true, to_apply=%region_1.2 | all-reduce | flops 10240 | bytes 81920 | tf_op jit(solution)/shard_map/psum | solution.py:161
  147.8 1.4 reduce_sum.73
  149.7 11.7 %cholesky.74 = f32[128,128]{1,0:T(8,128)S(1)} custom-call(f32[128,128]{1,0:T(8,128)S(1)} %copy.93), custom_call_target="Cholesky" | custom-call | tf_op jit(solution)/shard_map/jit(cholesky)/cholesky | solution.py:69
  162.1 0.7 select_bitcast_fusion.7
  162.8 9.8 %custom-call.36 = f32[1,128,128]{1,2,0:T(8,128)S(1)} custom-call(f32[1,128,128]{2,1,0:T(8,128)S(1)} %get-tuple-element.21), custom_call_target="InvertDiagBlocksLowerTriangular" | custom-call | tf_op jit(solution)/shard_map/triangular_solve/custom-call.3 | solution.py:76
  172.9 9.8 %custom-call.35 = f32[1,128,128]{1,2,0:T(8,128)S(1)} custom-call(f32[1,128,128]{2,1,0:T(8,128)S(1)} %get-tuple-element.20), custom_call_target="InvertDiagBlocksLowerTriangular" | custom-call | tf_op jit(solution)/shard_map/triangular_solve/custom-call.2 | solution.py:72
  183.2 2.6 fusion.31
  186.0 2.8 fusion.186
  189.8 0.8 gather_fusion.1
  191.3 33.4 %psum.58 = f32[128,80]{0,1:T(8,128)S(1)} all-reduce(f32[128,80]{0,1:T(8,128)S(1)} %broadcast_select_fusion.2), channel_id=1, replica_groups=mesh['mem'=4,'sub'=8] {'sub'}, use_global_device_ids=true, to_apply=%region_6.12 | all-reduce | flops 10240 | bytes 81920 | tf_op jit(solution)/shard_map/psum | solution.py:161
  224.7 10.5 %psum.59 = f32[128,80]{0,1:T(8,128)S(1)} all-reduce(f32[128,80]{0,1:T(8,128)S(1)} %psum.58), channel_id=1, replica_groups=mesh['mem'=4,'sub'=8] {'mem'}, use_global_device_ids=true, to_apply=%region_7.13 | all-reduce | flops 10240 | bytes 81920 | tf_op jit(solution)/shard_map/psum | solution.py:161
  235.7 11.7 %cholesky.85 = f32[128,128]{1,0:T(8,128)S(1)} custom-call(f32[128,128]{1,0:T(8,128)S(1)} %copy.98), custom_call_target="Cholesky" | custom-call | tf_op jit(solution)/shard_map/jit(cholesky)/cholesky | solution.py:69
  247.5 0.7 compare_reduce_fusion.2
  248.2 0.7 select_bitcast_fusion.5
  248.9 9.8 %custom-call.40 = f32[1,128,128]{1,2,0:T(8,128)S(1)} custom-call(f32[1,128,128]{2,1,0:T(8,128)S(1)} %get-tuple-element.19), custom_call_target="InvertDiagBlocksLowerTriangular" | custom-call | tf_op jit(solution)/shard_map/triangular_solve/custom-call.3 | solution.py:76
  258.9 9.8 %custom-call.39 = f32[1,128,128]{1,2,0:T(8,128)S(1)} custom-call(f32[1,128,128]{2,1,0:T(8,128)S(1)} %get-tuple-element.18), custom_call_target="InvertDiagBlocksLowerTriangular" | custom-call | tf_op jit(solution)/shard_map/triangular_solve/custom-call.2 | solution.py:72
  269.2 2.6 fusion.37
  272.0 1.9 fusion.187
  274.9 0.8 gather_fusion.2
  276.4 35.3 %psum.60 = f32[128,80]{0,1:T(8,128)S(1)} all-reduce(f32[128,80]{0,1:T(8,128)S(1)} %broadcast_select_fusion.1), channel_id=1, replica_groups=mesh['mem'=4,'sub'=8] {'sub'}, use_global_device_ids=true, to_apply=%region_10.16 | all-reduce | flops 10240 | bytes 81920 | tf_op jit(solution)/shard_map/psum | solution.py:161
  311.7 10.5 %psum.61 = f32[128,80]{0,1:T(8,128)S(1)} all-reduce(f32[128,80]{0,1:T(8,128)S(1)} %psum.60), channel_id=1, replica_groups=mesh['mem'=4,'sub'=8] {'mem'}, use_global_device_ids=true, to_apply=%region_11.17 | all-reduce | flops 10240 | bytes 81920 | tf_op jit(solution)/shard_map/psum | solution.py:161
  322.8 11.7 %cholesky.96 = f32[128,128]{1,0:T(8,128)S(1)} custom-call(f32[128,128]{1,0:T(8,128)S(1)} %copy.101), custom_call_target="Cholesky" | custom-call | tf_op jit(solution)/shard_map/jit(cholesky)/cholesky | solution.py:69
  334.6 0.7 compare_reduce_fusion.1
  335.2 0.7 select_bitcast_fusion.3
  335.9 9.8 %custom-call.44 = f32[1,128,128]{1,2,0:T(8,128)S(1)} custom-call(f32[1,128,128]{2,1,0:T(8,128)S(1)} %get-tuple-element.17), custom_call_target="InvertDiagBlocksLowerTriangular" | custom-call | tf_op jit(solution)/shard_map/triangular_solve/custom-call.3 | solution.py:76
  346.0 9.8 %custom-call.43 = f32[1,128,128]{1,2,0:T(8,128)S(1)} custom-call(f32[1,128,128]{2,1,0:T(8,128)S(1)} %get-tuple-element.16), custom_call_target="InvertDiagBlocksLowerTriangular" | custom-call | tf_op jit(solution)/shard_map/triangular_solve/custom-call.2 | solution.py:72
  356.2 2.6 fusion.35
  359.1 1.9 fusion.188
  362.0 0.8 gather_fusion.3
  363.5 33.4 %psum.62 = f32[128,80]{0,1:T(8,128)S(1)} all-reduce(f32[128,80]{0,1:T(8,128)S(1)} %broadcast_select_fusion), channel_id=1, replica_groups=mesh['mem'=4,'sub'=8] {'sub'}, use_global_device_ids=true, to_apply=%region_14.20 | all-reduce | flops 10240 | bytes 81920 | tf_op jit(solution)/shard_map/psum | solution.py:161
  396.8 10.5 %psum.63 = f32[128,80]{0,1:T(8,128)S(1)} all-reduce(f32[128,80]{0,1:T(8,128)S(1)} %psum.62), channel_id=1, replica_groups=mesh['mem'=4,'sub'=8] {'mem'}, use_global_device_ids=true, to_apply=%region_15.21 | all-reduce | flops 10240 | bytes 81920 | tf_op jit(solution)/shard_map/psum | solution.py:161
  407.9 11.7 %cholesky.107 = f32[128,128]{1,0:T(8,128)S(1)} custom-call(f32[128,128]{1,0:T(8,128)S(1)} %copy.104), custom_call_target="Cholesky" | custom-call | tf_op jit(solution)/shard_map/jit(cholesky)/cholesky | solution.py:69
  419.7 0.7 compare_reduce_fusion
  420.4 0.8 select_bitcast_fusion.1
  421.2 9.8 %custom-call.48 = f32[1,128,128]{1,2,0:T(8,128)S(1)} custom-call(f32[1,128,128]{2,1,0:T(8,128)S(1)} %get-tuple-element.15), custom_call_target="InvertDiagBlocksLowerTriangular" | custom-call | tf_op jit(solution)/shard_map/triangular_solve/custom-call.3 | solution.py:76
  431.2 9.8 %custom-call.47 = f32[1,128,128]{1,2,0:T(8,128)S(1)} custom-call(f32[1,128,128]{2,1,0:T(8,128)S(1)} %get-tuple-element.14), custom_call_target="InvertDiagBlocksLowerTriangular" | custom-call | tf_op jit(solution)/shard_map/triangular_solve/custom-call.2 | solution.py:72
  441.4 2.6 fusion.33
  444.3 1.7 fusion.20
  446.0 1.2 copy.105
  (133 shorter events, 14.2 us)
Async XLA Ops:
  0.0 14.1 %copy-start.8 = (f32[20,1,24,512]{3,2,1,0:T(8,128)S(1)}, f32[20,1,24,512]{3,2,1,0:T(8,128)}, u32[]{:S(2)}) copy-start(f32[20,1,24,512]{3,2,1,0:T(8,128)} %param.18) | copy-start | bytes 2949124
  0.0 47.4 %collective-permute-start = (f32[20,1,24,512]{3,2,1,0:T(8,128)}, f32[20,1,24,512]{3,2,1,0:T(8,128)}, u32[]{:S(2)}, u32[]{:S(2)}) collective-permute-start(f32[20,1,24,512]{3,2,1,0:T(8,128)} %param.18), channel_id=1, source_target_pairs={{0,1},{1,2},{2,3},{3,4},{4,5},{5,6},{6,7},{8,9},{9,10},{10,11},{11... | collective-permute-start | bytes 2949128 | tf_op jit(solution)/shard_map/ppermute | solution.py:16
  5.9 41.4 %collective-permute-start.1 = (f32[20,1,24,512]{3,2,1,0:T(8,128)}, f32[20,1,24,512]{3,2,1,0:T(8,128)S(1)}, u32[]{:S(2)}, u32[]{:S(2)}) collective-permute-start(f32[20,1,24,512]{3,2,1,0:T(8,128)} %param.18), channel_id=1, source_target_pairs={{1,0},{2,1},{3,2},{4,3},{5,4},{6,5},{7,6},{9,8},{10,9},{11,10},{12... | collective-permute-start | bytes 2949128 | tf_op jit(solution)/shard_map/ppermute | solution.py:17
  14.1 34.2 %copy-start.15 = (f32[1,512]{1,0:T(1,128)S(1)}, f32[1,512]{1,0:T(1,128)}, u32[]{:S(2)}) copy-start(f32[1,512]{1,0:T(1,128)} %param.21) | copy-start | bytes 6148
  47.4 0.9 copy-start.10
  61.5 6.4 %copy-start.28 = (f32[4,128]{1,0:T(4,128)S(1)}, f32[4,128]{1,0:T(4,128)}, u32[]{:S(2)}) copy-start(f32[4,128]{1,0:T(4,128)} %param.26) | copy-start | bytes 6148
  61.5 17.8 %all-to-all-start = ((f32[4,1,61440]{2,1,0:T(1,128)}), f32[4,1,61440]{2,1,0:T(1,128)S(1)}, u32[]{:S(2)}, u32[]{:S(2)}) async-start(f32[4,1,61440]{2,1,0:T(1,128)} %reshape.1524), calls=%async_computation | async-start | bytes 1966080 | tf_op jit(solution)/shard_map/all_to_all | solution.py:134
  94.9 0.9 copy-start.9
  95.9 1.0 copy-start.6
  97.7 1.5 copy-start.19
  97.7 51.5 %copy-start.27 = (f32[128]{0:T(128)S(1)}, f32[128]{0:T(128)}, u32[]{:S(2)}) copy-start(f32[128]{0:T(128)} %get-tuple-element.52) | copy-start | bytes 1540
  97.7 64.4 %copy-start.26 = (f32[128]{0:T(128)S(1)}, f32[128]{0:T(128)}, u32[]{:S(2)}) copy-start(f32[128]{0:T(128)} %get-tuple-element.49) | copy-start | bytes 1540
  99.1 83.6 %copy-start.13 = (f32[4,128]{1,0:T(4,128)S(1)}, f32[4,128]{1,0:T(4,128)}, u32[]{:S(2)}) copy-start(f32[4,128]{1,0:T(4,128)} %param.23) | copy-start | bytes 6148
  99.1 84.0 %copy-start.7 = (f32[4,20,1,24,128]{4,3,1,0,2:T(8,128)S(1)}, f32[4,20,1,24,128]{4,3,1,0,2:T(8,128)}, u32[]{:S(2)}) copy-start(f32[4,20,1,24,128]{4,3,1,0,2:T(8,128)} %copy-done.6) | copy-start | bytes 2949124
  188.8 0.9 copy-start.2
  189.8 0.8 copy-start.11
  190.6 0.7 copy-start.18
  190.6 44.6 %copy-start.25 = (f32[128]{0:T(128)S(1)}, f32[128]{0:T(128)}, u32[]{:S(2)}) copy-start(f32[128]{0:T(128)} %get-tuple-element.51) | copy-start | bytes 1540
  190.6 57.6 %copy-start.24 = (f32[128]{0:T(128)S(1)}, f32[128]{0:T(128)}, u32[]{:S(2)}) copy-start(f32[128]{0:T(128)} %get-tuple-element.48) | copy-start | bytes 1540
  190.6 78.5 %copy-start.12 = (f32[24,128]{1,0:T(8,128)S(1)}, f32[24,128]{1,0:T(8,128)}, u32[]{:S(2)}) copy-start(f32[24,128]{1,0:T(8,128)} %get-tuple-element.64) | copy-start | bytes 36868
  190.7 78.5 %copy-start.3 = (f32[80,24,128]{2,0,1:T(8,128)S(1)}, f32[80,24,128]{2,0,1:T(8,128)}, u32[]{:S(2)}) copy-start(f32[80,24,128]{2,0,1:T(8,128)} %copy-done.2) | copy-start | bytes 2949124
  273.9 0.9 copy-start.4
  275.7 0.7 copy-start.17
  275.7 46.6 %copy-start.23 = (f32[128]{0:T(128)S(1)}, f32[128]{0:T(128)}, u32[]{:S(2)}) copy-start(f32[128]{0:T(128)} %get-tuple-element.53) | copy-start | bytes 1540
  275.7 59.5 %copy-start.22 = (f32[128]{0:T(128)S(1)}, f32[128]{0:T(128)}, u32[]{:S(2)}) copy-start(f32[128]{0:T(128)} %get-tuple-element.47) | copy-start | bytes 1540
  275.8 80.4 %copy-start.5 = (f32[80,24,128]{2,0,1:T(8,128)S(1)}, f32[80,24,128]{2,0,1:T(8,128)}, u32[]{:S(2)}) copy-start(f32[80,24,128]{2,0,1:T(8,128)} %copy-done.4) | copy-start | bytes 2949124
  361.0 0.9 copy-start
  362.8 0.7 copy-start.16
  362.8 44.6 %copy-start.21 = (f32[128]{0:T(128)S(1)}, f32[128]{0:T(128)}, u32[]{:S(2)}) copy-start(f32[128]{0:T(128)} %get-tuple-element.50) | copy-start | bytes 1540
  362.8 57.6 %copy-start.20 = (f32[128]{0:T(128)S(1)}, f32[128]{0:T(128)}, u32[]{:S(2)}) copy-start(f32[128]{0:T(128)} %get-tuple-element.46) | copy-start | bytes 1540
  362.8 78.2 %copy-start.14 = (f32[4,128]{1,0:T(4,128)S(1)}, f32[4,128]{1,0:T(4,128)}, u32[]{:S(2)}) copy-start(f32[4,128]{1,0:T(4,128)} %param.23) | copy-start | bytes 6148
  362.8 78.5 %copy-start.1 = (f32[80,24,128]{2,0,1:T(8,128)S(1)}, f32[80,24,128]{2,0,1:T(8,128)}, u32[]{:S(2)}) copy-start(f32[80,24,128]{2,0,1:T(8,128)} %copy-done) | copy-start | bytes 2949124
